TPU v7x, 32 devices: a whole 2x2x4 slice. The times are simulated.
32 devices in a mesh: dp: 8 (over z, y), tp: 4 (over x, core).
Axes of the slice: x: 2, y: 2, z: 4, core: 2. Of those that a mesh axis runs over, the one named last changes fastest.
Arguments:
- attn_partial: bfloat16 [4, 512, 7168], P('tp', 'dp'), may hold values from -3 to 3
- hidden_in: bfloat16 [512, 7168], P('dp', 'tp'), may hold values from -6 to 6
- norm_gain: float32 [7168], replicated, may hold values from 0.5 to 1.5
- expert_ids: int32 [512, 8], P('dp'), may hold values from 0 to 255, all different within a row; in each aligned block of 64 rows (0 to 63, 64 to 127, ...) at most 4 rows name the same one
- route_prob: bfloat16 [512, 8], P('dp'), may hold values from 0.049804688 to 0.3984375
- w_gate: bfloat16 [8, 7168, 1024], P('dp', None, 'tp'), may hold values from -0.0625 to 0.0625
- w_up: bfloat16 [8, 7168, 1024], P('dp', None, 'tp'), may hold values from -0.0625 to 0.0625
- w_down: bfloat16 [8, 1024, 7168], P('dp', 'tp'), may hold values from -0.1875 to 0.1875
Outputs:
- layer_out: bfloat16 [512, 7168], P('dp', 'tp')
- amax_input: float32 [8], P('dp')
- amax_hidden: float32 [8], P('dp')
Inputs may be any that keep to these rules, and one draw needn't show every extreme that they name: `expert_ids`: each token names 8 different experts; within each aligned block of 64 tokens no expert is named by more than 4 tokens.
All inputs are finite; a program needn't handle non-finite values.
Results may differ from a plain program's by a relative error of at most 0.0075.
Values may be sent and summed in bfloat16 or wider, within the bound.
No kernel may reach another device: no remote copies, remote signals or barrier semaphores. Data moves between devices by JAX's collectives and lax.ppermute only.
A program may use at most 64 MiB of HBM per device.

v0:
```python
import jax
import jax.numpy as jnp
from jax import lax
from jax.sharding import PartitionSpec as P

EXPERT_SLOTS = 4
eps = 1e-06


def route_tables(expert_ids, route_prob, experts, capacity):
    matches = expert_ids[:, :, None] == jnp.arange(experts, dtype=jnp.int32)[None, None, :]
    onehot = jnp.sum(matches.astype(jnp.int32), axis=1)
    weight = jnp.sum(
        jnp.where(matches, route_prob[:, :, None].astype(jnp.float32), jnp.float32(0.0)), axis=1
    )
    before = jnp.cumsum(onehot, axis=0) - onehot
    placing = (onehot.T[:, None, :] == 1) & (
        before.T[:, None, :] == jnp.arange(capacity, dtype=jnp.int32)[None, :, None]
    )
    return (onehot, weight, placing)


def on_device(attn_partial, hidden_in, norm_gain, expert_ids, route_prob, w_gate, w_up, w_down):
    experts = lax.axis_size("dp")
    tp_index = lax.axis_index("tp")
    partial_value = attn_partial[0].astype(jnp.float32)
    token_count = partial_value.shape[0]
    columns = hidden_in.shape[1]
    start_col = tp_index * columns
    own_cols = lax.dynamic_slice_in_dim(partial_value, start_col, columns, 1) + hidden_in.astype(
        jnp.float32
    )
    summand = lax.dynamic_update_slice_in_dim(partial_value, own_cols, start_col, 1)
    residual = lax.psum(summand, "tp")
    mean_sq = jnp.mean(residual * residual, axis=1, keepdims=True)
    normed = (residual * lax.rsqrt(mean_sq + eps) * norm_gain).astype(jnp.bfloat16)
    residual_cols = lax.dynamic_slice_in_dim(residual, start_col, columns, 1)
    onehot, weight, placing = route_tables(expert_ids, route_prob, experts, EXPERT_SLOTS)
    selection_mask = placing.reshape(experts * EXPERT_SLOTS, token_count).astype(jnp.bfloat16)
    outgoing = jnp.dot(selection_mask, normed, preferred_element_type=jnp.float32).astype(
        jnp.bfloat16
    )
    piece_width = outgoing.shape[1]
    incoming = lax.all_to_all(
        outgoing.reshape(experts, EXPERT_SLOTS, piece_width),
        "dp",
        split_axis=0,
        concat_axis=0,
        tiled=True,
    )
    expert_slot_rows = incoming.reshape(experts * EXPERT_SLOTS, piece_width)
    gate_val = jnp.dot(expert_slot_rows, w_gate[0], preferred_element_type=jnp.float32)
    up_val = jnp.dot(expert_slot_rows, w_up[0], preferred_element_type=jnp.float32)
    hidden_act = (jax.nn.silu(gate_val) * up_val).astype(jnp.bfloat16)
    partial_out = jnp.dot(hidden_act, w_down[0], preferred_element_type=jnp.float32)
    combine_matrix = (placing.astype(jnp.float32) * weight.T[:, None, :]).reshape(
        experts * EXPERT_SLOTS, token_count
    )
    expert_cols = lax.psum_scatter(
        partial_out.astype(jnp.bfloat16), "tp", scatter_dimension=1, tiled=True
    ).astype(jnp.float32)
    returned = lax.all_to_all(
        expert_cols.reshape(experts, EXPERT_SLOTS, columns).astype(jnp.bfloat16),
        "dp",
        split_axis=0,
        concat_axis=0,
        tiled=True,
    ).astype(jnp.float32)
    moe_out = jnp.dot(
        combine_matrix.T,
        returned.reshape(experts * EXPERT_SLOTS, columns),
        precision=lax.Precision.HIGHEST,
        preferred_element_type=jnp.float32,
    )
    layer_out = (residual_cols + moe_out).astype(jnp.bfloat16)
    hidden_peak = jnp.max(jnp.abs(hidden_act.astype(jnp.float32)))
    input_peak = jnp.max(jnp.abs(expert_slot_rows.astype(jnp.float32)))
    input_peak, hidden_peak = lax.pmax((input_peak, hidden_peak), "tp")
    amax_input = input_peak.reshape(1)
    amax_hidden = hidden_peak.reshape(1)
    return (layer_out, amax_input, amax_hidden)


def solution(mesh):
    placed = (
        P("tp", "dp", None),
        P("dp", "tp"),
        P(),
        P("dp", None),
        P("dp", None),
        P("dp", None, "tp"),
        P("dp", None, "tp"),
        P("dp", "tp", None),
    )
    return jax.shard_map(
        on_device,
        mesh=mesh,
        in_specs=placed,
        out_specs=(P("dp", "tp"), P("dp"), P("dp")),
        check_vma=False,
    )
```

profile of v0, /device:TPU:0, one launch (start us, length us, event | category | flops | bytes accessed | tf_op | source)
XLA Modules:
  0.0 132.3 jit_solution(10730123870915161944)
XLA Ops:
  7.2 0.0 all-reduce.3.cloned.1.call-start
  7.2 0.0 copy-start.4
  7.2 2.8 %fusion.27 = (f32[1,64,7168]{2,1,0:T(8,128)}, f32[64,7168]{1,0:T(8,128)S(1)}) fusion(bf16[1,64,7168]{2,1,0:T(8,128)(2,1)} %param.8), kind=kLoop, calls=%fused_computation.38 | loop fusion | flops 458752 | bytes 4587520 | tf_op jit(solution)/shard_map/convert_element_type | solution.py:26
  10.1 0.0 copy-start.6
  10.1 0.0 copy-done.4
  10.1 1.1 fusion.15
  11.1 0.0 copy-start
  11.1 0.0 copy-start.5
  11.2 1.2 copy-done
  12.4 0.0 all-reduce.3.cloned.1.call-update
  12.4 0.0 reduce-scatter.2.cloned.1.call-start
  12.4 0.0 copy-done.6
  12.5 0.1 copy.26
  12.5 0.1 reduce_window_sum.11
  12.6 0.1 copy.28
  12.7 0.1 eq.58
  12.8 49.6 %all-reduce.3.cloned.1.call-done = f32[64,7168]{1,0:T(8,128)} async-done(((f32[64,7168]{1,0:T(8,128)}), f32[64,7168]{1,0:T(8,128)}) %all-reduce.3.cloned.1.call-update) | async-done | bytes 1835024 | tf_op jit(solution)/shard_map/psum | solution.py:34
  62.4 0.0 copy-start.1
  62.4 1.9 %multiply_reduce_fusion = f32[64]{0:T(128)S(1)} fusion(f32[64,7168]{1,0:T(8,128)} %all-reduce.3.cloned.1.call-done), kind=kLoop, calls=%fused_computation.11 | loop fusion | flops 917440 | bytes 1835264 | tf_op jit(solution)/shard_map/reduce_sum | solution.py:35
  64.3 0.0 copy-done.5
  64.3 0.1 copy-done.1
  64.4 0.4 convolution_convert_fusion.1
  64.8 0.2 reshape.44
  65.0 18.3 %all_to_all.10 = bf16[8,4,7168]{2,1,0:T(4,128)(2,1)S(1)} all-to-all(bf16[8,4,7168]{2,1,0:T(4,128)(2,1)S(1)} %reshape.44), channel_id=1, replica_groups=mesh['dp'=8,'tp'=4] {'dp'}, dimensions={0} | all-to-all | bytes 917504 | tf_op jit(solution)/shard_map/all_to_all | solution.py:44
  83.3 0.1 reshape.45
  83.4 0.0 copy-start.2
  83.4 2.9 %fusion.3 = f32[32,256]{1,0:T(8,128)S(1)} fusion(bf16[32,7168]{1,0:T(8,128)(2,1)S(1)} %reshape.45, bf16[1,7168,256]{2,1,0:T(8,128)(2,1)} %param.13), kind=kOutput, calls=%fused_computation.5 | convolution fusion | flops 117440512 | bytes 4161536 | tf_op jit(solution)/shard_map/dot_general | solution.py:52
  86.3 0.2 copy-done.2
  86.5 0.0 copy-start.3
  86.5 1.3 %abs_reduce_fusion.1 = (f32[]{:T(128)}, bf16[32,256]{1,0:T(8,128)(2,1)S(1)}) fusion(bf16[32,7168]{1,0:T(8,128)(2,1)S(1)} %reshape.45, bf16[1,7168,256]{2,1,0:T(8,128)(2,1)S(1)} %copy-done.2, f32[32,256]{1,0:T(8,128)S(1)} %fusion.3), kind=kOutput, calls=%fused_computation.20 | convolution fusion | flops 117514240 | bytes 4177924 | tf_op jit(solution)/shard_map/dot_general | solution.py:53
  87.9 0.7 copy-done.3
  88.6 0.0 copy-start.7
  88.6 1.5 %convolution_convert_fusion = bf16[32,7168]{1,0:T(8,128)(2,1)} fusion(bf16[32,256]{1,0:T(8,128)(2,1)S(1)} %get-tuple-element.8, bf16[1,256,7168]{2,1,0:T(8,128)(2,1)S(1)} %copy-done.3), kind=kOutput, calls=%fused_computation | convolution fusion | flops 117669888 | bytes 4145152 | tf_op jit(solution)/shard_map/dot_general | solution.py:55
  90.1 0.0 reduce-scatter.2.cloned.1.call-update
  90.1 0.0 copy-done.7
  90.1 19.5 %reduce-scatter.2.cloned.1.call-done = bf16[32,1792]{1,0:T(8,128)(2,1)} async-done(((bf16[32,7168]{1,0:T(8,128)(2,1)}), bf16[32,1792]{1,0:T(8,128)(2,1)}) %reduce-scatter.2.cloned.1.call-update) | async-done | bytes 114704 | tf_op jit(solution)/shard_map/reduce_scatter | solution.py:59
  109.7 1.6 %convert_element_type.55 = bf16[8,4,1792]{2,1,0:T(4,128)(2,1)} reshape(bf16[32,1792]{1,0:T(8,128)(2,1)} %reduce-scatter.2.cloned.1.call-done) | data formatting | bytes 229376 | tf_op jit(solution)/shard_map/convert_element_type | solution.py:63
  111.2 5.5 %all-to-all-start.1 = ((bf16[8,4,1792]{2,1,0:T(4,128)(2,1)}), bf16[8,4,1792]{2,1,0:T(4,128)(2,1)S(1)}, u32[]{:S(2)}, u32[]{:S(2)}) async-start(bf16[8,4,1792]{2,1,0:T(4,128)(2,1)} %convert_element_type.55), calls=%async_computation.2 | async-start | bytes 229376 | tf_op jit(solution)/shard_map/all_to_all | solution.py:62
  116.7 1.1 abs_reduce_fusion
  117.8 6.6 %all-reduce = (f32[1]{0:T(128)}, f32[1]{0:T(128)}) all-reduce(f32[1]{0:T(128)} %bitcast.11, f32[1]{0:T(128)} %bitcast.12), channel_id=1, replica_groups=mesh['dp'=8,'tp'=4] {'tp'}, use_global_device_ids=true, to_apply=%region_7.8 | all-reduce | flops 2 | bytes 16 | tf_op jit(solution)/shard_map/pmax | solution.py:78
  124.4 0.0 all-to-all-done.1
  124.4 1.1 fusion.6
  (9 shorter events, 0.1 us)
Async XLA Ops:
  7.2 55.2 %all-reduce.3.cloned.1.call-start = ((), (), s32[]{:S(2)}) async-start(), calls=%async_computation.3 | async-start | bytes 3670016 | tf_op jit(solution)/shard_map/psum | solution.py:34
  7.2 2.8 %copy-start.4 = (bf16[64,1792]{1,0:T(8,128)(2,1)S(1)}, bf16[64,1792]{1,0:T(8,128)(2,1)}, u32[]{:S(2)}) copy-start(bf16[64,1792]{1,0:T(8,128)(2,1)} %param.9) | copy-start | bytes 688132
  10.1 2.4 %copy-start.6 = (s32[64,8]{0,1:T(8,128)S(1)}, s32[64,8]{0,1:T(8,128)}, u32[]{:S(2)}) copy-start(s32[64,8]{0,1:T(8,128)} %param.11) | copy-start | bytes 6148
  11.1 1.2 copy-start
  11.1 53.1 %copy-start.5 = (f32[7168]{0:T(1024)S(1)}, f32[7168]{0:T(1024)}, u32[]{:S(2)}) copy-start(f32[7168]{0:T(1024)} %param.10) | copy-start | bytes 86020
  12.4 97.3 %reduce-scatter.2.cloned.1.call-start = ((), (), s32[]{:S(2)}) async-start(), calls=%async_computation.4 | async-start | bytes 573440 | tf_op jit(solution)/shard_map/reduce_scatter | solution.py:59
  62.4 2.1 %copy-start.1 = (f32[64,7168]{1,0:T(8,128)S(1)}, f32[64,7168]{1,0:T(8,128)}, u32[]{:S(2)}) copy-start(f32[64,7168]{1,0:T(8,128)} %all-reduce.3.cloned.1.call-done) | copy-start | bytes 5505028
  83.4 3.1 %copy-start.2 = (bf16[1,7168,256]{2,1,0:T(8,128)(2,1)S(1)}, bf16[1,7168,256]{2,1,0:T(8,128)(2,1)}, u32[]{:S(2)}) copy-start(bf16[1,7168,256]{2,1,0:T(8,128)(2,1)} %param.14) | copy-start | bytes 11010052
  86.5 2.0 %copy-start.3 = (bf16[1,256,7168]{2,1,0:T(8,128)(2,1)S(1)}, bf16[1,256,7168]{2,1,0:T(8,128)(2,1)}, u32[]{:S(2)}) copy-start(bf16[1,256,7168]{2,1,0:T(8,128)(2,1)} %param.15) | copy-start | bytes 11010052
  88.6 1.5 %copy-start.7 = (bf16[64,8]{0,1:T(8,128)(2,1)S(1)}, bf16[64,8]{0,1:T(8,128)(2,1)}, u32[]{:S(2)}) copy-start(bf16[64,8]{0,1:T(8,128)(2,1)} %param.12) | copy-start | bytes 3076
  111.2 13.2 %all-to-all-start.1 = ((bf16[8,4,1792]{2,1,0:T(4,128)(2,1)}), bf16[8,4,1792]{2,1,0:T(4,128)(2,1)S(1)}, u32[]{:S(2)}, u32[]{:S(2)}) async-start(bf16[8,4,1792]{2,1,0:T(4,128)(2,1)} %convert_element_type.55), calls=%async_computation.2 | async-start | bytes 229376 | tf_op jit(solution)/shard_map/all_to_all | solution.py:62
Sparse Core Ops, SparseCore 0:
  12.5 49.8 all-reduce.2
  90.2 19.3 reduce-scatter.1
where the time goes:
time: 133 us; the launch traced here: 132 us
  waiting for transfers between devices  69.1 us (52%)
  blocking collectives  24.9 us (19%)
  between operations  14.2 us (11%)
  matrix products  7.23 us (5%)
  other arithmetic  6.96 us (5%)
  starting transfers between devices  5.58 us (4%)
  local copies, waits for them, and re-layouts  4.39 us (3%)
    psum x1, waiting for transfers between devices, on_device(): residual = lax.psum(summand, 'tp')  49.6 us
    reduce_scatter x1, waiting for transfers between devices, on_device(): lax.psum_scatter(partial_out.astype(jnp.bfloat16), 'tp', scatter_dimensio...  19.5 us
    all_to_all x1, blocking collectives, on_device(): lax.all_to_all(outgoing.reshape(experts, EXPERT_SLOTS, piece_width), 'dp'...  18.3 us
    pmax x1, blocking collectives, on_device(): input_peak, hidden_peak = lax.pmax((input_peak, hidden_peak), 'tp')  6.59 us
    all_to_all x1, starting transfers between devices, on_device(): lax.all_to_all(expert_cols.reshape(experts, EXPERT_SLOTS, columns).astype...  5.5 us
    dot_general x1, matrix products, on_device(): jnp.dot(expert_slot_rows, w_gate[0], preferred_element_type=jnp.float32)  2.92 us
    convert_element_type x1, other arithmetic, on_device(): partial_value = attn_partial[0].astype(jnp.float32)  2.83 us
  transfers between devices with their start and end apart: 3, of which 2 were waited for; matrix products, arithmetic and copies ran while one was open for 1% of the time, Pallas kernels for 0%

commit v1 on v0

--- a/solution.py
+++ b/solution.py
@@ -31,7 +31,7 @@
         jnp.float32
     )
     summand = lax.dynamic_update_slice_in_dim(partial_value, own_cols, start_col, 1)
-    residual = lax.psum(summand, "tp")
+    residual = jnp.sum(lax.all_gather(summand, "tp"), axis=0)
     mean_sq = jnp.mean(residual * residual, axis=1, keepdims=True)
     normed = (residual * lax.rsqrt(mean_sq + eps) * norm_gain).astype(jnp.bfloat16)
     residual_cols = lax.dynamic_slice_in_dim(residual, start_col, columns, 1)

time: 133 us -> 138 us (1.038)
  waiting for transfers between devices: 69.1 us -> 74.1 us
    all_gather x0 -> x1, waiting for transfers between devices: none -> 54.8 us  [on_device(): residual = jnp.sum(lax.all_gather(summand, 'tp'), axis=0)]
    psum x1 -> x0, waiting for transfers between devices: 49.6 us -> none  [on_device(): residual = lax.psum(summand, 'tp')]
    reduce_sum x0 -> x1, other arithmetic: none -> 3.7 us  [on_device(): residual = jnp.sum(lax.all_gather(summand, 'tp'), axis=0)]
    reduce_sum x1, other arithmetic: 1.85 us -> 0.25 us  [on_device(): mean_sq = jnp.mean(residual * residual, axis=1, keepdims=True)]
    convert_element_type x1, other arithmetic: 2.83 us -> 1.34 us  [on_device(): partial_value = attn_partial[0].astype(jnp.float32)]
where the time goes in v1:
time: 138 us
  waiting for transfers between devices  74.1 us (54%)
  blocking collectives  25.5 us (18%)
  between operations  14.2 us (10%)
  matrix products  7.23 us (5%)
  other arithmetic  6.55 us (5%)
  starting transfers between devices  5.6 us (4%)
  local copies, waits for them, and re-layouts  4.85 us (4%)
    all_gather x1, waiting for transfers between devices, on_device(): residual = jnp.sum(lax.all_gather(summand, 'tp'), axis=0)  54.8 us
    reduce_scatter x1, waiting for transfers between devices, on_device(): lax.psum_scatter(partial_out.astype(jnp.bfloat16), 'tp', scatter_dimensio...  19.3 us
    all_to_all x1, blocking collectives, on_device(): lax.all_to_all(outgoing.reshape(experts, EXPERT_SLOTS, piece_width), 'dp'...  18.9 us
    pmax x1, blocking collectives, on_device(): input_peak, hidden_peak = lax.pmax((input_peak, hidden_peak), 'tp')  6.58 us
    all_to_all x1, starting transfers between devices, on_device(): lax.all_to_all(expert_cols.reshape(experts, EXPERT_SLOTS, columns).astype...  5.52 us
    reduce_sum x1, other arithmetic, on_device(): residual = jnp.sum(lax.all_gather(summand, 'tp'), axis=0)  3.7 us
    dot_general x1, matrix products, on_device(): jnp.dot(expert_slot_rows, w_gate[0], preferred_element_type=jnp.float32)  2.92 us
  transfers between devices with their start and end apart: 3, of which 2 were waited for; matrix products, arithmetic and copies ran while one was open for 1% of the time, Pallas kernels for 0%

profile of v1, /device:TPU:0, one launch (start us, length us, event | category | flops | bytes accessed | tf_op | source)
XLA Modules:
  0.0 138.1 jit_solution(9590424284655803030)
XLA Ops:
  7.2 0.0 all-gather.2.cloned.1.call-start
  7.2 0.0 copy-start.3
  7.2 1.3 convert_element_type.45
  8.6 0.0 copy-start.5
  8.6 0.0 copy-done.3
  8.6 0.1 bitcast_dynamic-update-slice_fusion
  8.7 0.0 copy-start
  8.7 1.3 copy-done
  10.0 0.0 all-gather.2.cloned.1.call-update
  10.0 0.0 reduce-scatter.2.cloned.1.call-start
  10.1 0.0 copy-done.5
  10.1 0.1 copy.26
  10.2 0.1 reduce_window_sum.11
  10.3 0.1 copy.28
  10.4 0.1 eq.58
  10.5 54.8 %all-gather.2.cloned.1.call-done = f32[4,64,7168]{2,1,0:T(8,128)} async-done(((f32[1,64,7168]{2,1,0:T(8,128)}), f32[4,64,7168]{2,1,0:T(8,128)}) %all-gather.2.cloned.1.call-update) | async-done | bytes 7340048 | tf_op jit(solution)/shard_map/all_gather | solution.py:34
  65.2 3.7 %reduce_sum.36 = f32[64,7168]{1,0:T(8,128)S(1)} reduce(f32[4,64,7168]{2,1,0:T(8,128)} %all-gather.2.cloned.1.call-done, f32[]{:T(128)} %constant.24.clone.1), dimensions={0}, to_apply=%region_0.0 | reduce | flops 1376256 | bytes 9175044 | tf_op jit(solution)/shard_map/reduce_sum | solution.py:34
  68.9 0.0 copy-start.4
  68.9 0.2 multiply_reduce_fusion
  69.2 0.5 copy-done.4
  69.7 0.4 convolution_convert_fusion.1
  70.1 0.2 reshape.46
  70.2 18.9 %all_to_all.10 = bf16[8,4,7168]{2,1,0:T(4,128)(2,1)S(1)} all-to-all(bf16[8,4,7168]{2,1,0:T(4,128)(2,1)S(1)} %reshape.46), channel_id=1, replica_groups=mesh['dp'=8,'tp'=4] {'dp'}, dimensions={0} | all-to-all | bytes 917504 | tf_op jit(solution)/shard_map/all_to_all | solution.py:44
  89.2 0.1 reshape.47
  89.3 0.0 copy-start.1
  89.3 2.9 %fusion.3 = f32[32,256]{1,0:T(8,128)S(1)} fusion(bf16[32,7168]{1,0:T(8,128)(2,1)S(1)} %reshape.47, bf16[1,7168,256]{2,1,0:T(8,128)(2,1)} %param.13), kind=kOutput, calls=%fused_computation.5 | convolution fusion | flops 117440512 | bytes 4161536 | tf_op jit(solution)/shard_map/dot_general | solution.py:52
  92.2 0.2 copy-done.1
  92.4 0.0 copy-start.2
  92.4 1.3 abs_reduce_fusion.1
  93.7 0.7 copy-done.2
  94.5 0.0 copy-start.6
  94.5 1.5 %convolution_convert_fusion = bf16[32,7168]{1,0:T(8,128)(2,1)} fusion(bf16[32,256]{1,0:T(8,128)(2,1)S(1)} %get-tuple-element.6, bf16[1,256,7168]{2,1,0:T(8,128)(2,1)S(1)} %copy-done.2), kind=kOutput, calls=%fused_computation | convolution fusion | flops 117669888 | bytes 4145152 | tf_op jit(solution)/shard_map/dot_general | solution.py:55
  96.0 0.0 reduce-scatter.2.cloned.1.call-update
  96.0 0.0 copy-done.6
  96.0 19.3 %reduce-scatter.2.cloned.1.call-done = bf16[32,1792]{1,0:T(8,128)(2,1)} async-done(((bf16[32,7168]{1,0:T(8,128)(2,1)}), bf16[32,1792]{1,0:T(8,128)(2,1)}) %reduce-scatter.2.cloned.1.call-update) | async-done | bytes 114704 | tf_op jit(solution)/shard_map/reduce_scatter | solution.py:59
  115.3 1.6 %convert_element_type.53 = bf16[8,4,1792]{2,1,0:T(4,128)(2,1)} reshape(bf16[32,1792]{1,0:T(8,128)(2,1)} %reduce-scatter.2.cloned.1.call-done) | data formatting | bytes 229376 | tf_op jit(solution)/shard_map/convert_element_type | solution.py:63
  116.9 5.5 %all-to-all-start.1 = ((bf16[8,4,1792]{2,1,0:T(4,128)(2,1)}), bf16[8,4,1792]{2,1,0:T(4,128)(2,1)S(1)}, u32[]{:S(2)}, u32[]{:S(2)}) async-start(bf16[8,4,1792]{2,1,0:T(4,128)(2,1)} %convert_element_type.53), calls=%async_computation.2 | async-start | bytes 229376 | tf_op jit(solution)/shard_map/all_to_all | solution.py:62
  122.5 1.1 abs_reduce_fusion
  123.5 6.6 %all-reduce = (f32[1]{0:T(128)}, f32[1]{0:T(128)}) all-reduce(f32[1]{0:T(128)} %bitcast.11, f32[1]{0:T(128)} %bitcast.12), channel_id=1, replica_groups=mesh['dp'=8,'tp'=4] {'tp'}, use_global_device_ids=true, to_apply=%region_7.8 | all-reduce | flops 2 | bytes 16 | tf_op jit(solution)/shard_map/pmax | solution.py:78
  130.1 0.0 all-to-all-done.1
  130.1 1.1 fusion.6
  (10 shorter events, 0.1 us)
Async XLA Ops:
  7.2 58.1 %all-gather.2.cloned.1.call-start = ((), (), s32[]{:S(2)}) async-start(), calls=%async_computation.3 | async-start | bytes 9175040 | tf_op jit(solution)/shard_map/all_gather | solution.py:34
  7.2 1.4 %copy-start.3 = (bf16[64,1792]{1,0:T(8,128)(2,1)S(1)}, bf16[64,1792]{1,0:T(8,128)(2,1)}, u32[]{:S(2)}) copy-start(bf16[64,1792]{1,0:T(8,128)(2,1)} %param.9) | copy-start | bytes 688132
  8.6 1.5 %copy-start.5 = (s32[64,8]{0,1:T(8,128)S(1)}, s32[64,8]{0,1:T(8,128)}, u32[]{:S(2)}) copy-start(s32[64,8]{0,1:T(8,128)} %param.11) | copy-start | bytes 6148
  8.7 1.3 copy-start
  10.0 105.3 %reduce-scatter.2.cloned.1.call-start = ((), (), s32[]{:S(2)}) async-start(), calls=%async_computation.4 | async-start | bytes 573440 | tf_op jit(solution)/shard_map/reduce_scatter | solution.py:59
  68.9 0.8 copy-start.4
  89.3 3.1 %copy-start.1 = (bf16[1,7168,256]{2,1,0:T(8,128)(2,1)S(1)}, bf16[1,7168,256]{2,1,0:T(8,128)(2,1)}, u32[]{:S(2)}) copy-start(bf16[1,7168,256]{2,1,0:T(8,128)(2,1)} %param.14) | copy-start | bytes 11010052
  92.4 2.0 %copy-start.2 = (bf16[1,256,7168]{2,1,0:T(8,128)(2,1)S(1)}, bf16[1,256,7168]{2,1,0:T(8,128)(2,1)}, u32[]{:S(2)}) copy-start(bf16[1,256,7168]{2,1,0:T(8,128)(2,1)} %param.15) | copy-start | bytes 11010052
  94.5 1.5 %copy-start.6 = (bf16[64,8]{0,1:T(8,128)(2,1)S(1)}, bf16[64,8]{0,1:T(8,128)(2,1)}, u32[]{:S(2)}) copy-start(bf16[64,8]{0,1:T(8,128)(2,1)} %param.12) | copy-start | bytes 3076
  116.9 13.2 %all-to-all-start.1 = ((bf16[8,4,1792]{2,1,0:T(4,128)(2,1)}), bf16[8,4,1792]{2,1,0:T(4,128)(2,1)S(1)}, u32[]{:S(2)}, u32[]{:S(2)}) async-start(bf16[8,4,1792]{2,1,0:T(4,128)(2,1)} %convert_element_type.53), calls=%async_computation.2 | async-start | bytes 229376 | tf_op jit(solution)/shard_map/all_to_all | solution.py:62
Sparse Core Ops, SparseCore 0:
  10.2 55.0 all-gather.1
  96.1 19.1 reduce-scatter.1
